TPU v7x, 256 devices: a whole 4x4x8 slice. The times are simulated.
256 devices in a mesh: chan: 64 (over y, x_lo, z), rep: 4 (over x_hi, core).
Axes of the slice: x: 4 (x_hi: 2, x_lo: 2; x = x_hi * 2 + x_lo), y: 4, z: 8, core: 2. Of those that a mesh axis runs over, the one named last changes fastest.
Arguments:
- records: bfloat16 [2, 64, 256, 2048], P(None, None, 'rep', 'chan'), may hold values from -6 to 6
- sources: int32 [128], replicated, may hold values from 0 to 16383
- dead_list: int32 [2, 1024], replicated, may hold values from 0 to 16383
Outputs:
- correlations: float32 [128, 64, 16384], P('rep', None, 'chan')
All inputs are finite; a program needn't handle non-finite values.
Results may differ from a plain program's by a relative error of at most 0.0072.
Values may be sent and summed in bfloat16 or wider, within the bound.
A program may use at most 64 MiB of HBM per device.

v0:
```python
import math
import jax
import jax.numpy as jnp
from jax import lax
from jax.sharding import PartitionSpec as P

WINDOW_SAMPLES = 2048
K = 256
K0 = 16
HALF = 32
WH = 32
LAGS = 64
tile_span = 128
tiny_eps = 1e-06


def live_table(dead_list, total):
    window_count, listed = dead_list.shape
    window_rows = jnp.broadcast_to(
        jnp.arange(window_count, dtype=jnp.int32)[:, None], (window_count, listed)
    )
    return jnp.ones((window_count, total), jnp.float32).at[window_rows, dead_list].set(0.0)


def running_mean(records):
    length = records.shape[-1]
    blocks = length // tile_span
    leading = records.shape[:-1]
    magnitude = jnp.abs(records)
    padded = jnp.pad(magnitude, [(0, 0)] * (records.ndim - 1) + [(tile_span, tile_span)])
    before = padded[..., :length].reshape(leading + (blocks, tile_span))
    middle = magnitude.reshape(leading + (blocks, tile_span))
    after = padded[..., 2 * tile_span :].reshape(leading + (blocks, tile_span))
    views = jnp.concatenate([before, middle, after], axis=-1).reshape(-1, 3 * tile_span)
    offsets = jnp.arange(3 * tile_span, dtype=jnp.int32)[:, None] - tile_span
    targets = jnp.arange(tile_span, dtype=jnp.int32)[None, :]
    band_unit_mask = (jnp.abs(offsets - targets) <= HALF).astype(jnp.bfloat16)
    totals = jnp.dot(views, band_unit_mask, preferred_element_type=jnp.float32).reshape(
        leading + (length,)
    )
    sample = jnp.arange(length, dtype=jnp.int32)
    counts = (jnp.minimum(sample, HALF) + jnp.minimum(length - 1 - sample, HALF) + 1).astype(
        jnp.float32
    )
    return totals / counts


def dft_table(length):
    sample = jnp.arange(length, dtype=jnp.int32)[:, None]
    bin_index = K0 + jnp.arange(K, dtype=jnp.int32)[None, :]
    phase = sample * bin_index % length
    angle = phase.astype(jnp.float32) * (2.0 * math.pi / length)
    return jnp.concatenate([jnp.cos(angle), -jnp.sin(angle)], axis=1).astype(jnp.bfloat16)


def whiten(spectrum):
    real_part = spectrum[:, :K]
    imag_part = spectrum[:, K:]
    amplitude = jnp.sqrt(real_part * real_part + imag_part * imag_part)
    index_row = jnp.arange(K, dtype=jnp.int32)[:, None]
    index_col = jnp.arange(K, dtype=jnp.int32)[None, :]
    band = (jnp.abs(index_row - index_col) <= WH).astype(jnp.float32)
    smoothed_amplitude = jnp.dot(amplitude, band, precision=lax.Precision.HIGHEST) / jnp.sum(
        band, axis=0
    )
    return (
        spectrum / (jnp.concatenate([smoothed_amplitude, smoothed_amplitude], axis=1) + tiny_eps)
    ).astype(jnp.bfloat16)


def preprocess(records):
    mean_abs = running_mean(records)
    normed = (records.astype(jnp.float32) / (mean_abs + tiny_eps)).astype(jnp.bfloat16)
    spectrum = jnp.dot(normed, dft_table(records.shape[-1]), preferred_element_type=jnp.float32)
    return whiten(spectrum)


def lag_kernel(source_spectrum):
    bin_index = K0 + jnp.arange(K, dtype=jnp.int32)[None, :]
    lag_index = jnp.arange(LAGS, dtype=jnp.int32)[:, None] - LAGS // 2
    phase = jnp.mod(lag_index * bin_index, WINDOW_SAMPLES)
    angle = phase.astype(jnp.float32) * (2.0 * math.pi / WINDOW_SAMPLES)
    cosine_lookup = jnp.cos(angle)[None, :, None, :]
    sin_table = jnp.sin(angle)[None, :, None, :]
    real_part = source_spectrum[:, None, :, :K].astype(jnp.float32)
    imag_part = source_spectrum[:, None, :, K:].astype(jnp.float32)
    with_real = real_part * cosine_lookup + imag_part * sin_table
    with_imag = imag_part * cosine_lookup - real_part * sin_table
    return jnp.concatenate([with_real, with_imag], axis=3).astype(jnp.bfloat16)


def correlate(kernel, spectra, source_live, chan_live):
    summed = lax.dot_general(
        kernel, spectra, (((2, 3), (0, 2)), ((), ())), preferred_element_type=jnp.float32
    )
    pairs = jnp.dot(source_live.T, chan_live, precision=lax.Precision.HIGHEST)
    return summed / (math.sqrt(K) * jnp.maximum(pairs, 1.0))[:, None, :]


def shards(records, sources, dead_list):
    window_count, groups, ch_width, span_len = records.shape
    reps = lax.axis_size("rep")
    chan_place = lax.axis_index("chan")
    rep_place = lax.axis_index("rep")
    group_share = ch_width * reps
    total = groups * group_share
    live = live_table(dead_list, total)
    group_ids = (
        jnp.arange(groups, dtype=jnp.int32)[:, None] * group_share
        + rep_place * ch_width
        + jnp.arange(ch_width, dtype=jnp.int32)[None, :]
    )
    live_here = live[:, group_ids]
    masked = jnp.where(live_here[..., None] > 0.5, records, jnp.zeros_like(records))
    arrived = lax.all_to_all(masked, "chan", split_axis=1, concat_axis=3, tiled=True)
    flat_rows = arrived.reshape(-1, arrived.shape[-1])
    spectra = preprocess(flat_rows).reshape(arrived.shape[0], ch_width, 2 * K)
    own_ids = (
        chan_place * group_share + rep_place * ch_width + jnp.arange(ch_width, dtype=jnp.int32)
    )
    onehot = (sources[:, None] == own_ids[None, :]).astype(jnp.bfloat16)
    picked = jnp.einsum("sc,wcf->swf", onehot, spectra, preferred_element_type=jnp.float32)
    quarter = sources.shape[0] // reps
    summed = lax.psum(picked, ("chan", "rep"))
    mine = lax.dynamic_slice_in_dim(summed, rep_place * quarter, quarter, 0)
    source_spectrum = mine.astype(jnp.bfloat16)
    source_live = live[:, sources]
    kernel = lag_kernel(source_spectrum)
    quarter_live = lax.dynamic_slice_in_dim(source_live, rep_place * quarter, quarter, 1)
    piece = lax.all_gather(spectra, "rep", axis=1, tiled=True)
    piece_ids = chan_place * group_share + jnp.arange(piece.shape[1], dtype=jnp.int32)
    return correlate(kernel, piece, quarter_live, live[:, piece_ids])


def solution(mesh):
    placed = (P(None, None, "rep", "chan"), P(), P())
    return jax.shard_map(
        shards, mesh=mesh, in_specs=placed, out_specs=P("rep", None, "chan"), check_vma=False
    )
```

profile of v0, /device:TPU:1, one launch (start us, length us, event | category | flops | bytes accessed | tf_op | source)
XLA Modules:
  0.0 189.5 jit_solution(2742913124565968528)
XLA Ops:
  0.0 0.7 fusion.51
  0.7 0.8 and_reduce_fusion
  1.5 0.7 multiply_reduce_fusion
  2.4 8.1 %scatter_custom_fusion = f32[32768]{0:T(1024)S(1)} fusion(s32[2048]{0:T(1024)S(1)} %bitcast.50, f32[2048]{0:T(1024)S(1)} %broadcast.257, f32[]{:T(128)} %constant.27.clone.1), kind=kCustom, calls=%fused_computation.68 | custom fusion | bytes 131076
  10.6 5.0 %copy.42 = f32[2,16384]{0,1:T(8,128)} copy(f32[2,16384]{1,0:T(2,128)S(1)} %reshape.212) | data formatting | bytes 262144 | tf_op jit(solution)/shard_map/scatter | solution.py:22
  15.6 14.1 %gather_fusion = f32[4096,2]{1,0:T(8,128)S(1)} fusion(f32[2,16384]{0,1:T(8,128)} %copy.42, s32[4096]{0:T(1024)S(1)} %broadcast_clamp_fusion), kind=kCustom, calls=%fused_computation | custom fusion | bytes 81920 | tf_op jit(solution)/shard_map/gather | solution.py:113
  30.0 0.7 copy.43
  30.7 1.4 fusion.59
  32.1 1.5 reshape.254
  33.6 13.8 %all-to-all-start = ((bf16[64,2,2048]{2,1,0:T(2,128)(2,1)}), bf16[64,2,2048]{2,1,0:T(2,128)(2,1)S(1)}, u32[]{:S(2)}, u32[]{:S(2)}) async-start(bf16[64,2,2048]{2,1,0:T(2,128)(2,1)} %reshape.254), calls=%async_computation | async-start | bytes 1048576 | tf_op jit(solution)/shard_map/all_to_all | solution.py:115
  47.6 4.0 %gather_fusion.1 = f32[128,2]{1,0:T(8,128)S(1)} fusion(f32[2,16384]{0,1:T(8,128)} %copy.42, s32[1024]{0:T(1024)S(1)} %pad_clamp_fusion.1), kind=kCustom, calls=%fused_computation.1 | custom fusion | bytes 2560 | tf_op jit(solution)/shard_map/gather | solution.py:127
  51.6 4.1 %gather_fusion.2 = f32[256,2]{1,0:T(8,128)S(1)} fusion(f32[2,16384]{0,1:T(8,128)} %copy.42, s32[1024]{0:T(1024)S(1)} %pad_clamp_fusion), kind=kCustom, calls=%fused_computation.2 | custom fusion | bytes 5120 | tf_op jit(solution)/shard_map/gather | solution.py:132
  56.3 9.4 %cosine_convert_fusion = (bf16[2048,256]{1,0:T(8,128)(2,1)}, bf16[2048,256]{1,0:T(8,128)(2,1)}) fusion(s32[256]{0:T(256)S(1)} %iota_add_fusion.1), kind=kLoop, calls=%fused_computation.23 | loop fusion | flops 8912896 | bytes 2098176 | tf_op jit(solution)/shard_map/convert.5
  65.7 0.7 reshape.255
  66.4 1.5 abs_bitcast_fusion
  67.9 2.1 %copy.46 = bf16[2,1,64,64,32]{2,0,4,3,1:T(2,128)(2,1)} copy(bf16[2,1,64,64,32]{2,4,0,3,1:T(8,128)(2,1)S(1)} %get-tuple-element.5) | data formatting | bytes 1048576 | tf_op jit(solution)/shard_map/abs | solution.py:29
  70.0 3.2 %copy.48 = bf16[2,1,64,64,32]{4,3,2,0,1:T(8,128)(2,1)S(1)} copy(bf16[2,1,64,64,32]{2,4,0,3,1:T(8,128)(2,1)S(1)} %get-tuple-element.5) | data formatting | bytes 1048576 | tf_op jit(solution)/shard_map/abs | solution.py:29
  73.2 4.9 %copy.45 = f32[2,1,64,64,32]{2,0,4,3,1:T(2,128)} copy(f32[2,1,64,64,32]{2,4,0,3,1:T(8,128)} %get-tuple-element.6) | data formatting | bytes 2097152 | tf_op jit(solution)/shard_map/convert_element_type | solution.py:73
  78.1 3.4 %reshape.213 = f32[128,2048]{0,1:T(8,128)} reshape(f32[2,1,64,64,32]{2,0,4,3,1:T(2,128)} %copy.45) | data formatting | bytes 2097152 | tf_op jit(solution)/shard_map/convert_element_type | solution.py:73
  81.5 1.3 abs.30
  82.8 1.2 pad_slice_fusion.1
  84.0 1.0 copy.47
  85.0 2.1 %concatenate.23 = bf16[2048,128]{1,0:T(8,128)(2,1)} reshape(bf16[128,2048]{1,0:T(8,128)(2,1)} %copy.47) | data formatting | bytes 1048576 | tf_op jit(solution)/shard_map/concatenate | solution.py:34
  87.3 1.1 concatenate.24
  88.4 1.7 abs.31
  90.1 2.0 %fusion.16 = f32[2048,128]{1,0:T(8,128)S(1)} fusion(bf16[2048,128]{1,0:T(8,128)(2,1)} %concatenate.24, bf16[2048,128]{1,0:T(8,128)(2,1)} %abs.31, bf16[2048,128]{1,0:T(8,128)(2,1)} %concatenate.23, s32[384]{0:T(512)S(1)} %iota_add_fusion), kind=kOutput, calls=%fused_computation.27 | convolution fusion | flops 206192640 | bytes 2622976 | tf_op jit(solution)/shard_map/dot_general | solution.py:38
  92.6 0.7 copy-done.1
  93.4 2.5 %fusion.7 = f32[128,512]{1,0:T(8,128)S(1)} fusion(bf16[2048,256]{1,0:T(8,128)(2,1)} %get-tuple-element.16, bf16[2048,256]{1,0:T(8,128)(2,1)} %get-tuple-element.15, f32[128,2048]{0,1:T(8,128)S(1)} %copy-done.1, f32[128,2048]{0,1:T(8,128)S(1)} %copy.50, f32[2048]{0:T(1024)S(1)} %fusion.49), kind=kOutput, calls=%fused_computation.16 | convolution fusion | flops 273678336 | bytes 4464640 | tf_op jit(solution)/shard_map/dot_general | solution.py:74
  96.2 9.4 %all_gather.3 = bf16[2,256,512]{2,1,0:T(8,128)(2,1)S(1)} all-gather(bf16[2,64,512]{2,1,0:T(8,128)(2,1)S(1)} %bitcast.48), channel_id=1, replica_groups=mesh['chan'=64,'rep'=4] {'rep'}, dimensions={1}, use_global_device_ids=true | all-gather | bytes 655360 | tf_op jit(solution)/shard_map/all_gather | solution.py:130
  106.0 79.2 %all-reduce.2 = bf16[128,2,512]{2,0,1:T(8,128)(2,1)S(1)} all-reduce(f32[128,2,512]{2,0,1:T(8,128)S(1)} %fusion.41), channel_id=1, replica_groups=mesh['chan'=64,'rep'=4] {'chan','rep'}, use_global_device_ids=true, to_apply=%region_2.3 | all-reduce | flops 131072 | bytes 786432 | tf_op jit(solution)/shard_map/psum | solution.py:124
  185.4 1.5 add_convert_fusion
  186.9 2.7 %bitcast_divide_fusion = f32[32,64,256]{2,1,0:T(8,128)} fusion(bf16[32,64,2,256]{3,1,2,0:T(8,128)(2,1)S(1)} %get-tuple-element.10, bf16[32,64,2,256]{3,1,2,0:T(8,128)(2,1)S(1)} %get-tuple-element.9, f32[32,256]{1,0:T(8,128)S(1)} %fusion.22, bf16[2,256,512]{2,1,0:T(8,128)(2,1)S(1)} %all_gather.3), kind=kOutput, calls=%fused_computation.21 | convolution fusion | flops 1082654720 | bytes 6848512 | tf_op jit(solution)/shard_map/dot_general | solution.py:93
  (38 shorter events, 2.7 us)
Async XLA Ops:
  30.7 16.8 %copy-start.2 = (s32[128]{0:T(128)S(1)}, s32[128]{0:T(128)}, u32[]{:S(2)}) copy-start(s32[128]{0:T(128)} %param.4) | copy-start | bytes 1540
  33.6 32.1 %all-to-all-start = ((bf16[64,2,2048]{2,1,0:T(2,128)(2,1)}), bf16[64,2,2048]{2,1,0:T(2,128)(2,1)S(1)}, u32[]{:S(2)}, u32[]{:S(2)}) async-start(bf16[64,2,2048]{2,1,0:T(2,128)(2,1)} %reshape.254), calls=%async_computation | async-start | bytes 1048576 | tf_op jit(solution)/shard_map/all_to_all | solution.py:115
  78.1 3.4 %copy-start = (bf16[2,1,64,64,32]{2,0,4,3,1:T(2,128)(2,1)S(1)}, bf16[2,1,64,64,32]{2,0,4,3,1:T(2,128)(2,1)}, u32[]{:S(2)}) copy-start(bf16[2,1,64,64,32]{2,0,4,3,1:T(2,128)(2,1)} %copy.46) | copy-start | bytes 1572868
  92.1 1.2 copy-start.1
where the time goes:
time: 190 us
  blocking collectives  88.6 us (47%)
  local copies, waits for them, and re-layouts  62 us (33%)
  other arithmetic  16.8 us (9%)
  starting transfers between devices  13.8 us (7%)
  matrix products  8.04 us (4%)
    psum x1, blocking collectives, shards(): summed = lax.psum(picked, ('chan', 'rep'))  79.2 us
    gather x1, local copies, waits for them, and re-layouts, shards(): live_here = live[:, group_ids]  14.1 us
    all_to_all x1, starting transfers between devices, shards(): lax.all_to_all(masked, 'chan', split_axis=1, concat_axis=3, tiled=True)  13.8 us
    unnamed x11, local copies, waits for them, and re-layouts  11 us
    another operation x2, other arithmetic  10.9 us
    all_gather x1, blocking collectives, shards(): piece = lax.all_gather(spectra, 'rep', axis=1, tiled=True)  9.42 us
    abs x4, local copies, waits for them, and re-layouts, running_mean(): magnitude = jnp.abs(records)  8.32 us
    convert_element_type x2, local copies, waits for them, and re-layouts, preprocess(): records.astype(jnp.float32) / (mean_abs + tiny_eps)  8.27 us
  transfers between devices with their start and end apart: 1, of which 0 were waited for; matrix products, arithmetic and copies ran while one was open for 10% of the time, Pallas kernels for 0%

commit v1 on v0

--- a/solution.py
+++ b/solution.py
@@ -121,7 +121,9 @@
     onehot = (sources[:, None] == own_ids[None, :]).astype(jnp.bfloat16)
     picked = jnp.einsum("sc,wcf->swf", onehot, spectra, preferred_element_type=jnp.float32)
     quarter = sources.shape[0] // reps
-    summed = lax.psum(picked, ("chan", "rep"))
+    summed = picked
+    for name in ("rep", "chan"):
+        summed = lax.psum(summed, name)
     mine = lax.dynamic_slice_in_dim(summed, rep_place * quarter, quarter, 0)
     source_spectrum = mine.astype(jnp.bfloat16)
     source_live = live[:, sources]

time: 190 us -> 470 us (2.47)
  the two profiles are of different devices: /device:TPU:1 before, /device:TPU:4 now
where the time goes in v1:
time: 470 us
  blocking collectives  321 us (68%)
  local copies, waits for them, and re-layouts  62.3 us (13%)
  waiting for transfers between devices  33.7 us (7%)
  other arithmetic  17 us (4%)
  between operations  13.7 us (3%)
  starting transfers between devices  12.8 us (3%)
  matrix products  8.83 us (2%)
    psum x1, blocking collectives, shards(): summed = lax.psum(summed, name)  313 us
    psum x1, waiting for transfers between devices, shards(): summed = lax.psum(summed, name)  29.3 us
    gather x1, local copies, waits for them, and re-layouts, shards(): live_here = live[:, group_ids]  14.1 us
    all_to_all x1, starting transfers between devices, shards(): lax.all_to_all(masked, 'chan', split_axis=1, concat_axis=3, tiled=True)  12.7 us
    unnamed x11, local copies, waits for them, and re-layouts  11 us
    another operation x2, other arithmetic  10.9 us
  transfers between devices with their start and end apart: 2, of which 2 were waited for; matrix products, arithmetic and copies ran while one was open for 4% of the time, Pallas kernels for 0%

profile of v1, /device:TPU:4, one launch (start us, length us, event | category | flops | bytes accessed | tf_op | source)
XLA Modules:
  0.0 469.5 jit_solution(15151965742052058018)
XLA Ops:
  7.2 0.8 and_reduce_fusion
  8.0 0.7 multiply_reduce_fusion
  8.9 8.1 %scatter_custom_fusion = f32[32768]{0:T(1024)S(1)} fusion(s32[2048]{0:T(1024)S(1)} %bitcast.50, f32[2048]{0:T(1024)S(1)} %broadcast.257, f32[]{:T(128)} %constant.27.clone.1), kind=kCustom, calls=%fused_computation.68 | custom fusion | bytes 131076
  17.1 5.0 %copy.42 = f32[2,16384]{0,1:T(8,128)} copy(f32[2,16384]{1,0:T(2,128)S(1)} %reshape.212) | data formatting | bytes 262144 | tf_op jit(solution)/shard_map/scatter | solution.py:22
  22.1 14.1 %gather_fusion = f32[4096,2]{1,0:T(8,128)S(1)} fusion(f32[2,16384]{0,1:T(8,128)} %copy.42, s32[4096]{0:T(1024)S(1)} %broadcast_clamp_fusion), kind=kCustom, calls=%fused_computation | custom fusion | bytes 81920 | tf_op jit(solution)/shard_map/gather | solution.py:113
  36.5 0.7 copy.43
  37.3 1.4 fusion.59
  38.6 1.5 reshape.254
  40.2 12.7 %all-to-all-start = ((bf16[64,2,2048]{2,1,0:T(2,128)(2,1)}), bf16[64,2,2048]{2,1,0:T(2,128)(2,1)S(1)}, u32[]{:S(2)}, u32[]{:S(2)}) async-start(bf16[64,2,2048]{2,1,0:T(2,128)(2,1)} %reshape.254), calls=%async_computation | async-start | bytes 1048576 | tf_op jit(solution)/shard_map/all_to_all | solution.py:115
  53.3 4.0 gather_fusion.1
  57.7 9.4 %cosine_convert_fusion = (bf16[2048,256]{1,0:T(8,128)(2,1)}, bf16[2048,256]{1,0:T(8,128)(2,1)}) fusion(s32[256]{0:T(256)S(1)} %iota_add_fusion.1), kind=kLoop, calls=%fused_computation.23 | loop fusion | flops 8912896 | bytes 2098176 | tf_op jit(solution)/shard_map/convert.5
  67.1 4.3 all-to-all-done
  72.1 1.5 abs_bitcast_fusion
  73.6 2.1 copy.46
  75.7 3.2 copy.48
  79.0 4.9 %copy.45 = f32[2,1,64,64,32]{2,0,4,3,1:T(2,128)} copy(f32[2,1,64,64,32]{2,4,0,3,1:T(8,128)} %get-tuple-element.6) | data formatting | bytes 2097152 | tf_op jit(solution)/shard_map/convert_element_type | solution.py:73
  83.9 3.4 reshape.213
  87.3 1.3 abs.30
  88.6 1.3 pad_slice_fusion.1
  89.9 1.1 copy.47
  91.0 2.1 concatenate.23
  93.3 1.1 concatenate.24
  94.4 1.7 abs.31
  96.2 2.0 fusion.16
  99.4 2.5 fusion.7
  102.3 1.1 fusion.41
  103.4 4.1 gather_fusion.2
  107.8 8.4 %all_gather.3 = bf16[2,256,512]{2,1,0:T(8,128)(2,1)S(1)} all-gather(bf16[2,64,512]{2,1,0:T(8,128)(2,1)S(1)} %bitcast.49), channel_id=1, replica_groups=mesh['chan'=64,'rep'=4] {'rep'}, dimensions={1}, use_global_device_ids=true | all-gather | bytes 655360 | tf_op jit(solution)/shard_map/all_gather | solution.py:132
  116.2 29.3 %all-reduce.4.cloned.1.call-done = f32[128,2,512]{2,0,1:T(8,128)} async-done(((f32[128,2,512]{2,0,1:T(8,128)}), f32[128,2,512]{2,0,1:T(8,128)}) %all-reduce.4.cloned.1.call-update) | async-done | bytes 524304 | tf_op jit(solution)/shard_map/psum | solution.py:126
  145.5 312.8 %all-reduce.5 = bf16[128,2,512]{2,0,1:T(8,128)(2,1)S(1)} all-reduce(f32[128,2,512]{2,0,1:T(8,128)} %all-reduce.4.cloned.1.call-done), channel_id=1, replica_groups=mesh['chan'=64,'rep'=4] {'chan'}, use_global_device_ids=true, to_apply=%region_3.4 | all-reduce | flops 131072 | bytes 786432 | tf_op jit(solution)/shard_map/psum | solution.py:126
  458.5 1.5 add_convert_fusion
  460.0 2.7 bitcast_divide_fusion
  (41 shorter events, 4.7 us)
Async XLA Ops:
  37.2 16.0 %copy-start.2 = (s32[128]{0:T(128)S(1)}, s32[128]{0:T(128)}, u32[]{:S(2)}) copy-start(s32[128]{0:T(128)} %param.4) | copy-start | bytes 1540
  40.2 31.2 %all-to-all-start = ((bf16[64,2,2048]{2,1,0:T(2,128)(2,1)}), bf16[64,2,2048]{2,1,0:T(2,128)(2,1)S(1)}, u32[]{:S(2)}, u32[]{:S(2)}) async-start(bf16[64,2,2048]{2,1,0:T(2,128)(2,1)} %reshape.254), calls=%async_computation | async-start | bytes 1048576 | tf_op jit(solution)/shard_map/all_to_all | solution.py:115
  52.9 92.6 %all-reduce.4.cloned.1.call-start = ((), (), s32[]{:S(2)}) async-start(), calls=%async_computation.1 | async-start | bytes 1048576 | tf_op jit(solution)/shard_map/psum | solution.py:126
  83.9 3.4 copy-start
  98.2 1.2 copy-start.1
Sparse Core Ops, SparseCore 0:
  103.5 41.8 all-reduce.3
